TPU v7x, 32 devices: a whole 2x2x4 slice. The times are simulated.
32 devices in a mesh: walk: 2 (over core), det: 4 (over y, x), exc: 4 (over z).
Axes of the slice: x: 2, y: 2, z: 4, core: 2. Of those that a mesh axis runs over, the one named last changes fastest.
Arguments:
- inverse: bfloat16 [128, 128, 128], P(('walk', 'det', 'exc')), may hold values from -0.5 to 0.5
- virt_ref: bfloat16 [128, 128], replicated, may hold values from -6 to 6
- new_rows: bfloat16 [128, 128], P(('walk', 'det', 'exc')), may hold values from -6 to 6
- moved_electron: int32 [128], P(('walk', 'det', 'exc')), may hold values from 0 to 127
- coefficient: float32 [16384], P(('det', 'exc')), may hold values from -0.046875 to 0.046875
- occ_list: int32 [4, 16384], P(None, ('det', 'exc')), may hold values from 0 to 127
- virt_list: int32 [4, 16384], P(None, ('det', 'exc')), may hold values from 0 to 127
- exc_rank: int32 [16384], P(('det', 'exc')), may hold values from 1 to 4
Outputs:
- amplitude: float32 [128], P(('walk', 'det', 'exc'))
- ci_grad: float32 [16384], P(('det', 'exc'))
- orb_grad: float32 [128, 128], P('walk')
All inputs are finite; a program needn't handle non-finite values.
Results may differ from a plain program's by a relative error of at most 0.0015.
The roundings to bfloat16 on the way count: a program that leaves them out, or rounds other values in their place, can miss the bound.
Values may be sent and summed in bfloat16 or wider, within the bound.
No kernel may reach another device: no remote copies, remote signals or barrier semaphores. Data moves between devices by JAX's collectives and lax.ppermute only.
A program may use at most 64 MiB of HBM per device.

v0:
```python
import math
import jax
import jax.numpy as jnp
from jax import lax
from jax.sharding import PartitionSpec as P


def minor_det(cells):
    top_a = cells[0] * cells[5] - cells[4] * cells[1]
    top_b = cells[0] * cells[6] - cells[4] * cells[2]
    top_c = cells[0] * cells[7] - cells[4] * cells[3]
    top_d = cells[1] * cells[6] - cells[5] * cells[2]
    top_e = cells[1] * cells[7] - cells[5] * cells[3]
    top_f = cells[2] * cells[7] - cells[6] * cells[3]
    low_f = cells[10] * cells[15] - cells[14] * cells[11]
    low_e = cells[9] * cells[15] - cells[13] * cells[11]
    low_d = cells[9] * cells[14] - cells[13] * cells[10]
    low_c = cells[8] * cells[15] - cells[12] * cells[11]
    low_b = cells[8] * cells[14] - cells[12] * cells[10]
    low_a = cells[8] * cells[13] - cells[12] * cells[9]
    return (
        top_a * low_f
        - top_b * low_e
        + top_c * low_d
        + top_d * low_c
        - top_e * low_b
        + top_f * low_a
    )


def build_minor(entries, exc_rank):
    cells = []
    for row_pos in range(4):
        for col_pos in range(4):
            inside = (exc_rank > row_pos) & (exc_rank > col_pos)
            filler = jnp.float32(1.0 if row_pos == col_pos else 0.0)
            cells.append(jnp.where(inside[None, :], entries[:, row_pos * 4 + col_pos, :], filler))
    return cells


def select_entries(tables, occ_list, virt_list):
    walkers, nocc, nvirt = tables.shape
    count = occ_list.shape[1]
    width = math.gcd(count, max(128, 8192 // walkers))
    steps_count = count // width
    occ_blocks = occ_list.reshape(4, steps_count, width).transpose(1, 0, 2)
    virt_blocks = virt_list.reshape(4, steps_count, width).transpose(1, 0, 2)
    rows_iota = jnp.arange(nocc, dtype=jnp.int32)
    cols_iota = jnp.arange(nvirt, dtype=jnp.int32)

    def one_block(lists):
        occ_part, virt_part = lists
        virt_hot = (cols_iota[:, None, None] == virt_part[None, :, :]).astype(jnp.bfloat16)
        columns = jnp.einsum("wpv,vbi->wpbi", tables, virt_hot, preferred_element_type=jnp.float32)
        picked = []
        for slot in range(4):
            hit = rows_iota[:, None] == occ_part[slot][None, :]
            picked.append(jnp.sum(jnp.where(hit[None, :, None, :], columns, 0.0), axis=1))
        return jnp.stack(picked, axis=1).reshape(walkers, 16, width)

    gathered = lax.map(one_block, (occ_blocks, virt_blocks))
    return gathered.transpose(1, 2, 0, 3).reshape(walkers, 16, count)


def orbital_grad(weighted, occ_list, virt_list, nocc, nvirt):
    count = occ_list.shape[1]
    slots = weighted.reshape(4, 4, count)
    rows_iota = jnp.arange(nocc, dtype=jnp.int32)
    spread = jnp.zeros((nocc, 4, count), jnp.float32)
    for slot in range(4):
        hit = rows_iota[:, None, None] == occ_list[slot][None, None, :]
        spread = spread + jnp.where(hit, slots[slot][None, :, :], 0.0)
    virt_hot = (jnp.arange(nvirt, dtype=jnp.int32)[:, None, None] == virt_list[None, :, :]).astype(
        jnp.float32
    )
    return jnp.einsum("pbi,qbi->pq", spread, virt_hot, precision=lax.Precision.HIGHEST)


def ratios_and_puller(entries, exc_rank):
    return jax.vjp(lambda values: minor_det(build_minor(values, exc_rank)), entries)


def per_device(
    inverse, virt_ref, new_rows, moved_electron, coefficient, occ_list, virt_list, exc_rank
):
    nocc = inverse.shape[1]
    nvirt = virt_ref.shape[1]
    tab_count = inverse.shape[0]
    displaced = jnp.arange(nocc, dtype=jnp.int32)[None, :, None] == moved_electron[:, None, None]
    basis = jnp.where(displaced, new_rows[:, None, :], virt_ref[None, :, :])
    tables = jnp.einsum("wji,wiv->wjv", inverse, basis, preferred_element_type=jnp.float32).astype(
        jnp.bfloat16
    )
    total_walkers = tab_count * lax.axis_size("walk") * lax.axis_size(("det", "exc"))
    entries = select_entries(
        lax.all_gather(tables, ("det", "exc"), axis=0, tiled=True), occ_list, virt_list
    )
    ratios, puller = ratios_and_puller(entries, exc_rank)
    partial_value = jnp.dot(ratios, coefficient, precision=lax.Precision.HIGHEST)
    amplitude = 1.0 + lax.psum(partial_value, ("det", "exc"))
    weight = amplitude / (amplitude * amplitude + 1.0)
    grad_part = jnp.dot(weight, ratios, precision=lax.Precision.HIGHEST)
    cof_sum = jnp.sum(puller(jnp.broadcast_to(weight[:, None], ratios.shape))[0], axis=0)
    amp_mine = lax.dynamic_slice_in_dim(
        amplitude, lax.axis_index(("det", "exc")) * tab_count, tab_count, 0
    )
    ci_grad = lax.psum(grad_part, "walk") / total_walkers
    weighted = cof_sum * coefficient[None, :] / total_walkers
    orbital = orbital_grad(weighted, occ_list, virt_list, nocc, nvirt)
    summed = lax.psum(orbital, ("walk", "det", "exc"))
    share = nocc // lax.axis_size("walk")
    orb_grad = lax.dynamic_slice_in_dim(summed, lax.axis_index("walk") * share, share, 0)
    return (amp_mine, ci_grad, orb_grad)


def solution(mesh):
    return jax.shard_map(
        per_device,
        mesh=mesh,
        in_specs=(
            P(("walk", "det", "exc"), None, None),
            P(),
            P(("walk", "det", "exc"), None),
            P(("walk", "det", "exc")),
            P(("det", "exc")),
            P(None, ("det", "exc")),
            P(None, ("det", "exc")),
            P(("det", "exc")),
        ),
        out_specs=(P(("walk", "det", "exc")), P(("det", "exc")), P("walk", None)),
        check_vma=False,
    )
```

profile of v0, /device:TPU:1, one launch (start us, length us, event | category | flops | bytes accessed | tf_op | source)
XLA Modules:
  0.0 351.5 jit_solution(1757928485655057289)
XLA Ops:
  7.2 0.8 iota_compare_fusion.13
  8.0 0.9 copy.99
  8.9 0.9 fusion.19
  9.8 0.8 copy.100
  10.7 0.7 fusion.43
  11.4 0.9 fusion.46
  12.3 0.9 iota_compare_fusion.9
  13.2 0.8 iota_compare_fusion.11
  14.0 59.2 %all-gather.2.cloned.1.call-done = bf16[64,128,128]{2,1,0:T(8,128)(2,1)} async-done(((bf16[4,128,128]{2,1,0:T(8,128)(2,1)}), bf16[64,128,128]{2,1,0:T(8,128)(2,1)}) %all-gather.2.cloned.1.call-update) | async-done | bytes 2097168 | tf_op jit(solution)/shard_map/all_gather | solution.py:96
  73.2 89.1 %while.13 = (s32[]{:T(128)}, f32[8,64,16,128]{3,1,2,0:T(8,128)}, s32[8,4,128]{2,1,0:T(4,128)}, s32[8,4,128]{2,1,0:T(4,128)}, bf16[64,128,128]{2,1,0:T(8,128)(2,1)}, /*index=5*/s32[]{:T(128)}) while((s32[]{:T(128)}, f32[8,64,16,128]{3,1,2,0:T(8,128)}, s32[8,4,128]{2,1,0:T(4,128)}, s32[8,4,128]{2,1,0:T(4,128)}, ...), condition=%wide.region_5.6_spmd.clone.clone, body=%wide.region_0.5_spmd.clone.clone.sunk | while | flops 1107689472 | bytes 4866137 | solution.py:61
  73.2 0.7 constant_dynamic-slice_fusion.3
  74.0 0.7 dynamic-slice_bitcast_fusion.2
  74.7 8.8 %fusion.54 = (f32[64,4,128]{2,0,1:T(8,128)S(1)}, f32[64,4,128]{2,0,1:T(8,128)S(1)}, f32[64,4,128]{2,0,1:T(8,128)S(1)}, f32[64,4,128]{2,0,1:T(8,128)S(1)}) fusion(pred[128,128]{1,0:T(8,128)(4,1)S(1)} %get-tuple-element.237, pred[128,128]{1,0:T(8,128)(4,1)S(1)} %get-tuple-element.238, pred[128,128]{1,0:T(8,128)(4,1)S(1)} %get-tuple-element.241, ...), kind=kOutput, calls=%fused_computation.5.clone.1 | convolution fusion | flops 1107230720 | bytes 2689024 | tf_op jit(solution)/shard_map/while/body/eval_jaxpr/wpv,vbi->wpbi/dot_general | solution.py:54
  83.5 0.8 constant_dynamic-update-slice_fusion.2
  84.3 0.7 constant_dynamic-slice_fusion.3
  85.1 0.7 dynamic-slice_bitcast_fusion.2
  85.8 8.8 %fusion.54 = (f32[64,4,128]{2,0,1:T(8,128)S(1)}, f32[64,4,128]{2,0,1:T(8,128)S(1)}, f32[64,4,128]{2,0,1:T(8,128)S(1)}, f32[64,4,128]{2,0,1:T(8,128)S(1)}) fusion(pred[128,128]{1,0:T(8,128)(4,1)S(1)} %get-tuple-element.237, pred[128,128]{1,0:T(8,128)(4,1)S(1)} %get-tuple-element.238, pred[128,128]{1,0:T(8,128)(4,1)S(1)} %get-tuple-element.241, ...), kind=kOutput, calls=%fused_computation.5.clone.1 | convolution fusion | flops 1107230720 | bytes 2689024 | tf_op jit(solution)/shard_map/while/body/eval_jaxpr/wpv,vbi->wpbi/dot_general | solution.py:54
  94.6 0.8 constant_dynamic-update-slice_fusion.2
  95.5 0.7 constant_dynamic-slice_fusion.3
  96.2 0.7 dynamic-slice_bitcast_fusion.2
  96.9 8.8 %fusion.54 = (f32[64,4,128]{2,0,1:T(8,128)S(1)}, f32[64,4,128]{2,0,1:T(8,128)S(1)}, f32[64,4,128]{2,0,1:T(8,128)S(1)}, f32[64,4,128]{2,0,1:T(8,128)S(1)}) fusion(pred[128,128]{1,0:T(8,128)(4,1)S(1)} %get-tuple-element.237, pred[128,128]{1,0:T(8,128)(4,1)S(1)} %get-tuple-element.238, pred[128,128]{1,0:T(8,128)(4,1)S(1)} %get-tuple-element.241, ...), kind=kOutput, calls=%fused_computation.5.clone.1 | convolution fusion | flops 1107230720 | bytes 2689024 | tf_op jit(solution)/shard_map/while/body/eval_jaxpr/wpv,vbi->wpbi/dot_general | solution.py:54
  105.8 0.9 constant_dynamic-update-slice_fusion.2
  106.6 0.7 constant_dynamic-slice_fusion.3
  107.4 0.7 dynamic-slice_bitcast_fusion.2
  108.1 8.8 %fusion.54 = (f32[64,4,128]{2,0,1:T(8,128)S(1)}, f32[64,4,128]{2,0,1:T(8,128)S(1)}, f32[64,4,128]{2,0,1:T(8,128)S(1)}, f32[64,4,128]{2,0,1:T(8,128)S(1)}) fusion(pred[128,128]{1,0:T(8,128)(4,1)S(1)} %get-tuple-element.237, pred[128,128]{1,0:T(8,128)(4,1)S(1)} %get-tuple-element.238, pred[128,128]{1,0:T(8,128)(4,1)S(1)} %get-tuple-element.241, ...), kind=kOutput, calls=%fused_computation.5.clone.1 | convolution fusion | flops 1107230720 | bytes 2689024 | tf_op jit(solution)/shard_map/while/body/eval_jaxpr/wpv,vbi->wpbi/dot_general | solution.py:54
  116.9 0.9 constant_dynamic-update-slice_fusion.2
  117.8 0.7 constant_dynamic-slice_fusion.3
  118.5 0.7 dynamic-slice_bitcast_fusion.2
  119.2 8.8 %fusion.54 = (f32[64,4,128]{2,0,1:T(8,128)S(1)}, f32[64,4,128]{2,0,1:T(8,128)S(1)}, f32[64,4,128]{2,0,1:T(8,128)S(1)}, f32[64,4,128]{2,0,1:T(8,128)S(1)}) fusion(pred[128,128]{1,0:T(8,128)(4,1)S(1)} %get-tuple-element.237, pred[128,128]{1,0:T(8,128)(4,1)S(1)} %get-tuple-element.238, pred[128,128]{1,0:T(8,128)(4,1)S(1)} %get-tuple-element.241, ...), kind=kOutput, calls=%fused_computation.5.clone.1 | convolution fusion | flops 1107230720 | bytes 2689024 | tf_op jit(solution)/shard_map/while/body/eval_jaxpr/wpv,vbi->wpbi/dot_general | solution.py:54
  128.1 0.8 constant_dynamic-update-slice_fusion.2
  128.9 0.7 constant_dynamic-slice_fusion.3
  129.7 0.7 dynamic-slice_bitcast_fusion.2
  130.4 8.8 %fusion.54 = (f32[64,4,128]{2,0,1:T(8,128)S(1)}, f32[64,4,128]{2,0,1:T(8,128)S(1)}, f32[64,4,128]{2,0,1:T(8,128)S(1)}, f32[64,4,128]{2,0,1:T(8,128)S(1)}) fusion(pred[128,128]{1,0:T(8,128)(4,1)S(1)} %get-tuple-element.237, pred[128,128]{1,0:T(8,128)(4,1)S(1)} %get-tuple-element.238, pred[128,128]{1,0:T(8,128)(4,1)S(1)} %get-tuple-element.241, ...), kind=kOutput, calls=%fused_computation.5.clone.1 | convolution fusion | flops 1107230720 | bytes 2689024 | tf_op jit(solution)/shard_map/while/body/eval_jaxpr/wpv,vbi->wpbi/dot_general | solution.py:54
  139.2 0.8 constant_dynamic-update-slice_fusion.2
  140.0 0.7 constant_dynamic-slice_fusion.3
  140.8 0.7 dynamic-slice_bitcast_fusion.2
  141.5 8.8 %fusion.54 = (f32[64,4,128]{2,0,1:T(8,128)S(1)}, f32[64,4,128]{2,0,1:T(8,128)S(1)}, f32[64,4,128]{2,0,1:T(8,128)S(1)}, f32[64,4,128]{2,0,1:T(8,128)S(1)}) fusion(pred[128,128]{1,0:T(8,128)(4,1)S(1)} %get-tuple-element.237, pred[128,128]{1,0:T(8,128)(4,1)S(1)} %get-tuple-element.238, pred[128,128]{1,0:T(8,128)(4,1)S(1)} %get-tuple-element.241, ...), kind=kOutput, calls=%fused_computation.5.clone.1 | convolution fusion | flops 1107230720 | bytes 2689024 | tf_op jit(solution)/shard_map/while/body/eval_jaxpr/wpv,vbi->wpbi/dot_general | solution.py:54
  150.3 0.8 constant_dynamic-update-slice_fusion.2
  151.2 0.7 constant_dynamic-slice_fusion.3
  151.9 0.7 dynamic-slice_bitcast_fusion.2
  152.6 8.8 %fusion.54 = (f32[64,4,128]{2,0,1:T(8,128)S(1)}, f32[64,4,128]{2,0,1:T(8,128)S(1)}, f32[64,4,128]{2,0,1:T(8,128)S(1)}, f32[64,4,128]{2,0,1:T(8,128)S(1)}) fusion(pred[128,128]{1,0:T(8,128)(4,1)S(1)} %get-tuple-element.237, pred[128,128]{1,0:T(8,128)(4,1)S(1)} %get-tuple-element.238, pred[128,128]{1,0:T(8,128)(4,1)S(1)} %get-tuple-element.241, ...), kind=kOutput, calls=%fused_computation.5.clone.1 | convolution fusion | flops 1107230720 | bytes 2689024 | tf_op jit(solution)/shard_map/while/body/eval_jaxpr/wpv,vbi->wpbi/dot_general | solution.py:54
  161.5 0.8 constant_dynamic-update-slice_fusion.2
  162.3 2.8 copy_bitcast_fusion
  165.1 1.9 copy-done.1
  167.0 0.6 multiply_add_fusion
  167.9 32.4 %psum.21 = f32[64]{0:T(128)S(1)} all-reduce(f32[64]{0:T(128)S(1)} %convolution_bitcast_fusion), channel_id=1, replica_groups=mesh['walk'=2,'det'=4,'exc'=4] {'det','exc'}, use_global_device_ids=true, to_apply=%region_6.7 | all-reduce | flops 64 | bytes 512 | tf_op jit(solution)/shard_map/psum | solution.py:100
  200.3 0.5 fusion.40
  200.8 0.8 fusion.37
  201.6 1.9 add_select_fusion.7
  203.6 1.9 add_select_fusion.15
  205.5 0.4 add_select_fusion.6
  205.9 0.3 add_select_fusion.5
  206.7 0.4 add_select_fusion.14
  207.1 0.3 add_select_fusion.13
  207.4 1.0 add_select_fusion.9
  208.5 1.0 add_select_fusion.12
  209.4 1.7 add_select_fusion.11
  211.2 10.6 %psum.22 = f32[1024]{0:T(1024)S(1)} all-reduce(f32[1024]{0:T(1024)} %bitcast.162), channel_id=1, replica_groups=mesh['walk'=2,'det'=4,'exc'=4] {'walk'}, use_global_device_ids=true, to_apply=%region_7.8 | all-reduce | flops 1024 | bytes 8192 | tf_op jit(solution)/shard_map/psum | solution.py:107
  221.8 2.3 add_reduce_fusion
  224.3 2.8 fusion.20
  227.1 0.6 broadcast_multiply_fusion
  227.7 0.6 dynamic_slice.15
  228.3 115.0 %all-reduce.18.cloned.1.call-done = f32[128,128]{1,0:T(8,128)} async-done(((f32[128,128]{1,0:T(8,128)}), f32[128,128]{1,0:T(8,128)}) %all-reduce.18.cloned.1.call-update) | async-done | bytes 65552 | tf_op jit(solution)/shard_map/psum | solution.py:110
  343.3 1.4 constant_dynamic-slice_fusion.1
  (72 shorter events, 1.8 us)
Async XLA Ops:
  7.2 1.7 copy-start
  7.2 66.0 %all-gather.2.cloned.1.call-start = ((), (), s32[]{:S(2)}) async-start(), calls=%async_computation | async-start | bytes 2228224 | tf_op jit(solution)/shard_map/all_gather | solution.py:96
  10.6 332.7 %all-reduce.18.cloned.1.call-start = ((), (), s32[]{:S(2)}) async-start(), calls=%async_computation.1 | async-start | bytes 131072 | tf_op jit(solution)/shard_map/psum | solution.py:110
  11.4 195.7 %copy-start.8 = (pred[1024]{0:T(1024)(128)(4,1)}, pred[1024]{0:T(1024)(128)(4,1)S(1)}, u32[]{:S(2)}) copy-start(pred[1024]{0:T(1024)(128)(4,1)S(1)} %get-tuple-element.145) | copy-start | bytes 3076
  11.4 196.0 %copy-start.10 = (pred[1024]{0:T(1024)(128)(4,1)}, pred[1024]{0:T(1024)(128)(4,1)S(1)}, u32[]{:S(2)}) copy-start(pred[1024]{0:T(1024)(128)(4,1)S(1)} %get-tuple-element.179) | copy-start | bytes 3076
  11.4 196.0 %copy-start.7 = (pred[1024]{0:T(1024)(128)(4,1)}, pred[1024]{0:T(1024)(128)(4,1)S(1)}, u32[]{:S(2)}) copy-start(pred[1024]{0:T(1024)(128)(4,1)S(1)} %get-tuple-element.184) | copy-start | bytes 3076
  165.1 2.0 copy-start.1
  165.1 2.5 copy-start.11
  200.3 5.2 %copy-start.2 = (f32[64,16,1024]{2,0,1:T(8,128)S(1)}, f32[64,16,1024]{2,0,1:T(8,128)}, u32[]{:S(2)}) copy-start(f32[64,16,1024]{2,0,1:T(8,128)} %copy-done.1) | copy-start | bytes 12582916
  207.4 2.0 copy-start.9
  209.4 14.8 %copy-start.12 = (f32[1024]{0:T(1024)S(1)}, f32[1024]{0:T(1024)}, u32[]{:S(2)}) copy-start(f32[1024]{0:T(1024)} %param.14) | copy-start | bytes 12292
  221.8 2.4 copy-start.3
  221.8 2.5 copy-start.4
  221.8 2.5 copy-start.5
  221.8 2.5 copy-start.6
  221.8 2.5 copy-start.13
  224.2 3.5 %copy-start.14 = (f32[64]{0:T(128)S(1)}, f32[64]{0:T(128)}, u32[]{:S(2)}) copy-start(f32[64]{0:T(128)} %get-tuple-element.187) | copy-start | bytes 772
Sparse Core Ops, SparseCore 0:
  10.8 62.3 all-gather.1
  227.2 116.0 all-reduce.17
where the time goes:
time: 353 us; the launch traced here: 352 us
  waiting for transfers between devices  174 us (49%)
  matrix products  75.2 us (21%)
  blocking collectives  43 us (12%)
  local copies, waits for them, and re-layouts  27 us (8%)
  other arithmetic  17.4 us (5%)
  between operations  14.3 us (4%)
    psum x1, waiting for transfers between devices, per_device(): summed = lax.psum(orbital, ('walk', 'det', 'exc'))  115 us
    dot_general x8, matrix products, one_block(): jnp.einsum('wpv,vbi->wpbi', tables, virt_hot, preferred_element_type=jnp....  70.4 us
    all_gather x1, waiting for transfers between devices, per_device(): lax.all_gather(tables, ('det', 'exc'), axis=0, tiled=True)  59.2 us
    psum x1, blocking collectives, per_device(): amplitude = 1.0 + lax.psum(partial_value, ('det', 'exc'))  32.4 us
    psum x1, blocking collectives, per_device(): ci_grad = lax.psum(grad_part, 'walk') / total_walkers  10.6 us
    select_n x11, other arithmetic, build_minor(): jnp.where(inside[None, :], entries[:, row_pos * 4 + col_pos, :], filler)  9.44 us
  transfers between devices with their start and end apart: 2, of which 2 were waited for; matrix products, arithmetic and copies ran while one was open for 1% of the time, Pallas kernels for 0%

commit v1 on v0

--- a/solution.py
+++ b/solution.py
@@ -107,7 +107,7 @@
     ci_grad = lax.psum(grad_part, "walk") / total_walkers
     weighted = cof_sum * coefficient[None, :] / total_walkers
     orbital = orbital_grad(weighted, occ_list, virt_list, nocc, nvirt)
-    summed = lax.psum(orbital, ("walk", "det", "exc"))
+    summed = jnp.sum(lax.all_gather(orbital, ("walk", "det", "exc")), axis=0)
     share = nocc // lax.axis_size("walk")
     orb_grad = lax.dynamic_slice_in_dim(summed, lax.axis_index("walk") * share, share, 0)
     return (amp_mine, ci_grad, orb_grad)

time: 353 us -> 283 us (0.80)
  waiting for transfers between devices: 174 us -> 111 us
  other arithmetic: 17.4 us -> 12.9 us
    psum x1 -> x0, waiting for transfers between devices: 115 us -> none  [per_device(): summed = lax.psum(orbital, ('walk', 'det', 'exc'))]
    all_gather x0 -> x1, waiting for transfers between devices: none -> 49.9 us  [per_device(): summed = jnp.sum(lax.all_gather(orbital, ('walk', 'det', 'exc')), axis=0)]
where the time goes in v1:
time: 283 us; the launch traced here: 282 us
  waiting for transfers between devices  111 us (39%)
  matrix products  74.6 us (26%)
  blocking collectives  43.1 us (15%)
  local copies, waits for them, and re-layouts  26.2 us (9%)
  between operations  14.3 us (5%)
  other arithmetic  12.9 us (5%)
    dot_general x8, matrix products, one_block(): jnp.einsum('wpv,vbi->wpbi', tables, virt_hot, preferred_element_type=jnp....  70.4 us
    all_gather x1, waiting for transfers between devices, per_device(): lax.all_gather(tables, ('det', 'exc'), axis=0, tiled=True)  60.7 us
    all_gather x1, waiting for transfers between devices, per_device(): summed = jnp.sum(lax.all_gather(orbital, ('walk', 'det', 'exc')), axis=0)  49.9 us
    psum x1, blocking collectives, per_device(): amplitude = 1.0 + lax.psum(partial_value, ('det', 'exc'))  32.6 us
    psum x1, blocking collectives, per_device(): ci_grad = lax.psum(grad_part, 'walk') / total_walkers  10.5 us
    select_n x11, other arithmetic, build_minor(): jnp.where(inside[None, :], entries[:, row_pos * 4 + col_pos, :], filler)  6.84 us
    dynamic_update_slice x8, local copies, waits for them, and re-layouts, select_entries(): gathered = lax.map(one_block, (occ_blocks, virt_blocks))  6.76 us
  transfers between devices with their start and end apart: 2, of which 2 were waited for; matrix products, arithmetic and copies ran while one was open for 1% of the time, Pallas kernels for 0%

profile of v1, /device:TPU:1, one launch (start us, length us, event | category | flops | bytes accessed | tf_op | source)
XLA Modules:
  0.0 282.0 jit_solution(17178978555759305684)
XLA Ops:
  7.2 0.8 iota_compare_fusion.13
  8.0 0.9 copy.99
  8.9 0.9 fusion.19
  9.8 0.8 copy.100
  10.7 0.7 fusion.43
  11.4 0.9 fusion.46
  12.6 60.7 %all-gather.4.cloned.1.call-done = bf16[64,128,128]{2,1,0:T(8,128)(2,1)} async-done(((bf16[4,128,128]{2,1,0:T(8,128)(2,1)}), bf16[64,128,128]{2,1,0:T(8,128)(2,1)}) %all-gather.4.cloned.1.call-update) | async-done | bytes 2097168 | tf_op jit(solution)/shard_map/all_gather | solution.py:96
  73.2 89.1 %while.13 = (s32[]{:T(128)}, f32[8,64,16,128]{3,1,2,0:T(8,128)}, s32[8,4,128]{2,1,0:T(4,128)}, s32[8,4,128]{2,1,0:T(4,128)}, bf16[64,128,128]{2,1,0:T(8,128)(2,1)}, /*index=5*/s32[]{:T(128)}) while((s32[]{:T(128)}, f32[8,64,16,128]{3,1,2,0:T(8,128)}, s32[8,4,128]{2,1,0:T(4,128)}, s32[8,4,128]{2,1,0:T(4,128)}, ...), condition=%wide.region_5.6_spmd.clone.clone, body=%wide.region_0.5_spmd.clone.clone.sunk | while | flops 1107689472 | bytes 4866137 | solution.py:61
  73.2 0.7 constant_dynamic-slice_fusion.3
  74.0 0.7 dynamic-slice_bitcast_fusion.2
  74.7 8.8 %fusion.54 = (f32[64,4,128]{2,0,1:T(8,128)S(1)}, f32[64,4,128]{2,0,1:T(8,128)S(1)}, f32[64,4,128]{2,0,1:T(8,128)S(1)}, f32[64,4,128]{2,0,1:T(8,128)S(1)}) fusion(pred[128,128]{1,0:T(8,128)(4,1)S(1)} %get-tuple-element.237, pred[128,128]{1,0:T(8,128)(4,1)S(1)} %get-tuple-element.238, pred[128,128]{1,0:T(8,128)(4,1)S(1)} %get-tuple-element.241, ...), kind=kOutput, calls=%fused_computation.5.clone.1 | convolution fusion | flops 1107230720 | bytes 2689024 | tf_op jit(solution)/shard_map/while/body/eval_jaxpr/wpv,vbi->wpbi/dot_general | solution.py:54
  83.5 0.8 constant_dynamic-update-slice_fusion.2
  84.3 0.7 constant_dynamic-slice_fusion.3
  85.1 0.7 dynamic-slice_bitcast_fusion.2
  85.8 8.8 %fusion.54 = (f32[64,4,128]{2,0,1:T(8,128)S(1)}, f32[64,4,128]{2,0,1:T(8,128)S(1)}, f32[64,4,128]{2,0,1:T(8,128)S(1)}, f32[64,4,128]{2,0,1:T(8,128)S(1)}) fusion(pred[128,128]{1,0:T(8,128)(4,1)S(1)} %get-tuple-element.237, pred[128,128]{1,0:T(8,128)(4,1)S(1)} %get-tuple-element.238, pred[128,128]{1,0:T(8,128)(4,1)S(1)} %get-tuple-element.241, ...), kind=kOutput, calls=%fused_computation.5.clone.1 | convolution fusion | flops 1107230720 | bytes 2689024 | tf_op jit(solution)/shard_map/while/body/eval_jaxpr/wpv,vbi->wpbi/dot_general | solution.py:54
  94.6 0.8 constant_dynamic-update-slice_fusion.2
  95.5 0.7 constant_dynamic-slice_fusion.3
  96.2 0.7 dynamic-slice_bitcast_fusion.2
  96.9 8.8 %fusion.54 = (f32[64,4,128]{2,0,1:T(8,128)S(1)}, f32[64,4,128]{2,0,1:T(8,128)S(1)}, f32[64,4,128]{2,0,1:T(8,128)S(1)}, f32[64,4,128]{2,0,1:T(8,128)S(1)}) fusion(pred[128,128]{1,0:T(8,128)(4,1)S(1)} %get-tuple-element.237, pred[128,128]{1,0:T(8,128)(4,1)S(1)} %get-tuple-element.238, pred[128,128]{1,0:T(8,128)(4,1)S(1)} %get-tuple-element.241, ...), kind=kOutput, calls=%fused_computation.5.clone.1 | convolution fusion | flops 1107230720 | bytes 2689024 | tf_op jit(solution)/shard_map/while/body/eval_jaxpr/wpv,vbi->wpbi/dot_general | solution.py:54
  105.7 0.9 constant_dynamic-update-slice_fusion.2
  106.6 0.7 constant_dynamic-slice_fusion.3
  107.4 0.7 dynamic-slice_bitcast_fusion.2
  108.1 8.8 %fusion.54 = (f32[64,4,128]{2,0,1:T(8,128)S(1)}, f32[64,4,128]{2,0,1:T(8,128)S(1)}, f32[64,4,128]{2,0,1:T(8,128)S(1)}, f32[64,4,128]{2,0,1:T(8,128)S(1)}) fusion(pred[128,128]{1,0:T(8,128)(4,1)S(1)} %get-tuple-element.237, pred[128,128]{1,0:T(8,128)(4,1)S(1)} %get-tuple-element.238, pred[128,128]{1,0:T(8,128)(4,1)S(1)} %get-tuple-element.241, ...), kind=kOutput, calls=%fused_computation.5.clone.1 | convolution fusion | flops 1107230720 | bytes 2689024 | tf_op jit(solution)/shard_map/while/body/eval_jaxpr/wpv,vbi->wpbi/dot_general | solution.py:54
  116.9 0.8 constant_dynamic-update-slice_fusion.2
  117.8 0.7 constant_dynamic-slice_fusion.3
  118.5 0.7 dynamic-slice_bitcast_fusion.2
  119.2 8.8 %fusion.54 = (f32[64,4,128]{2,0,1:T(8,128)S(1)}, f32[64,4,128]{2,0,1:T(8,128)S(1)}, f32[64,4,128]{2,0,1:T(8,128)S(1)}, f32[64,4,128]{2,0,1:T(8,128)S(1)}) fusion(pred[128,128]{1,0:T(8,128)(4,1)S(1)} %get-tuple-element.237, pred[128,128]{1,0:T(8,128)(4,1)S(1)} %get-tuple-element.238, pred[128,128]{1,0:T(8,128)(4,1)S(1)} %get-tuple-element.241, ...), kind=kOutput, calls=%fused_computation.5.clone.1 | convolution fusion | flops 1107230720 | bytes 2689024 | tf_op jit(solution)/shard_map/while/body/eval_jaxpr/wpv,vbi->wpbi/dot_general | solution.py:54
  128.1 0.8 constant_dynamic-update-slice_fusion.2
  128.9 0.7 constant_dynamic-slice_fusion.3
  129.7 0.7 dynamic-slice_bitcast_fusion.2
  130.3 8.8 %fusion.54 = (f32[64,4,128]{2,0,1:T(8,128)S(1)}, f32[64,4,128]{2,0,1:T(8,128)S(1)}, f32[64,4,128]{2,0,1:T(8,128)S(1)}, f32[64,4,128]{2,0,1:T(8,128)S(1)}) fusion(pred[128,128]{1,0:T(8,128)(4,1)S(1)} %get-tuple-element.237, pred[128,128]{1,0:T(8,128)(4,1)S(1)} %get-tuple-element.238, pred[128,128]{1,0:T(8,128)(4,1)S(1)} %get-tuple-element.241, ...), kind=kOutput, calls=%fused_computation.5.clone.1 | convolution fusion | flops 1107230720 | bytes 2689024 | tf_op jit(solution)/shard_map/while/body/eval_jaxpr/wpv,vbi->wpbi/dot_general | solution.py:54
  139.2 0.8 constant_dynamic-update-slice_fusion.2
  140.0 0.7 constant_dynamic-slice_fusion.3
  140.8 0.7 dynamic-slice_bitcast_fusion.2
  141.5 8.8 %fusion.54 = (f32[64,4,128]{2,0,1:T(8,128)S(1)}, f32[64,4,128]{2,0,1:T(8,128)S(1)}, f32[64,4,128]{2,0,1:T(8,128)S(1)}, f32[64,4,128]{2,0,1:T(8,128)S(1)}) fusion(pred[128,128]{1,0:T(8,128)(4,1)S(1)} %get-tuple-element.237, pred[128,128]{1,0:T(8,128)(4,1)S(1)} %get-tuple-element.238, pred[128,128]{1,0:T(8,128)(4,1)S(1)} %get-tuple-element.241, ...), kind=kOutput, calls=%fused_computation.5.clone.1 | convolution fusion | flops 1107230720 | bytes 2689024 | tf_op jit(solution)/shard_map/while/body/eval_jaxpr/wpv,vbi->wpbi/dot_general | solution.py:54
  150.3 0.9 constant_dynamic-update-slice_fusion.2
  151.2 0.7 constant_dynamic-slice_fusion.3
  151.9 0.7 dynamic-slice_bitcast_fusion.2
  152.6 8.8 %fusion.54 = (f32[64,4,128]{2,0,1:T(8,128)S(1)}, f32[64,4,128]{2,0,1:T(8,128)S(1)}, f32[64,4,128]{2,0,1:T(8,128)S(1)}, f32[64,4,128]{2,0,1:T(8,128)S(1)}) fusion(pred[128,128]{1,0:T(8,128)(4,1)S(1)} %get-tuple-element.237, pred[128,128]{1,0:T(8,128)(4,1)S(1)} %get-tuple-element.238, pred[128,128]{1,0:T(8,128)(4,1)S(1)} %get-tuple-element.241, ...), kind=kOutput, calls=%fused_computation.5.clone.1 | convolution fusion | flops 1107230720 | bytes 2689024 | tf_op jit(solution)/shard_map/while/body/eval_jaxpr/wpv,vbi->wpbi/dot_general | solution.py:54
  161.5 0.8 constant_dynamic-update-slice_fusion.2
  162.3 2.8 copy_bitcast_fusion
  165.1 1.9 copy-done.1
  167.0 0.6 multiply_add_fusion
  167.6 0.3 convolution_bitcast_fusion
  167.9 32.6 %psum.14 = f32[64]{0:T(128)S(1)} all-reduce(f32[64]{0:T(128)S(1)} %convolution_bitcast_fusion), channel_id=1, replica_groups=mesh['walk'=2,'det'=4,'exc'=4] {'det','exc'}, use_global_device_ids=true, to_apply=%region_6.7 | all-reduce | flops 64 | bytes 512 | tf_op jit(solution)/shard_map/psum | solution.py:100
  200.5 2.1 add_select_fusion.7
  202.6 1.9 add_select_fusion.15
  204.5 0.4 add_select_fusion.6
  204.9 0.3 add_select_fusion.5
  205.2 0.3 add_select_fusion.3
  205.5 0.3 add_select_fusion.4
  205.8 0.4 add_select_fusion.14
  206.2 0.3 add_select_fusion.13
  206.5 0.4 add_select_fusion.9
  206.8 0.3 add_select_fusion.12
  207.1 0.3 add_select_fusion.11
  207.4 0.7 add_reduce_fusion
  208.1 2.8 %fusion.20 = f32[128,128]{1,0:T(8,128)} fusion(s32[4,1024]{1,0:T(4,128)S(1)} %bitcast.170, f32[4,1024]{1,0:T(4,128)S(1)} %get-tuple-element.168, f32[4,1024]{1,0:T(4,128)S(1)} %get-tuple-element.169, f32[4,1024]{1,0:T(4,128)S(1)} %get-tuple-element.170, f32[4,1024]{1,0:T(4,128)S(1)} %get-tuple-element.167, pred[128,1024]{1,0:T(8,128)(4,1)S(1)} %get-tuple-element.188, ...), kind=kOutput, calls=%fused_computation.39 | convolution fusion | flops 809500672 | bytes 671744 | tf_op jit(solution)/shard_map/pbi,qbi->pq/dot_general | solution.py:76
  211.0 0.6 dynamic_slice.15
  211.8 10.5 %psum.15 = f32[1024]{0:T(1024)S(1)} all-reduce(f32[1024]{0:T(1024)S(1)} %bitcast.164), channel_id=1, replica_groups=mesh['walk'=2,'det'=4,'exc'=4] {'walk'}, use_global_device_ids=true, to_apply=%region_7.8 | all-reduce | flops 1024 | bytes 8192 | tf_op jit(solution)/shard_map/psum | solution.py:107
  222.3 0.6 broadcast_multiply_fusion
  222.9 49.9 %all-gather.6.cloned.1.call-done = f32[4096,128]{1,0:T(8,128)} async-done(((f32[128,128]{1,0:T(8,128)}), f32[4096,128]{1,0:T(8,128)}) %all-gather.6.cloned.1.call-update) | async-done | bytes 2097168 | tf_op jit(solution)/shard_map/all_gather | solution.py:110
  272.8 1.7 reduce_sum.59
  274.5 0.6 constant_dynamic-slice_fusion.1
  (53 shorter events, 1.5 us)
Async XLA Ops:
  7.2 1.7 copy-start
  7.2 66.0 %all-gather.4.cloned.1.call-start = ((), (), s32[]{:S(2)}) async-start(), calls=%async_computation | async-start | bytes 2228224 | tf_op jit(solution)/shard_map/all_gather | solution.py:96
  10.6 262.2 %all-gather.6.cloned.1.call-start = ((), (), s32[]{:S(2)}) async-start(), calls=%async_computation.1 | async-start | bytes 2162688 | tf_op jit(solution)/shard_map/all_gather | solution.py:110
  165.1 2.0 copy-start.1
  165.1 2.5 copy-start.3
  200.5 4.0 %copy-start.2 = (f32[64,16,1024]{2,0,1:T(8,128)S(1)}, f32[64,16,1024]{2,0,1:T(8,128)}, u32[]{:S(2)}) copy-start(f32[64,16,1024]{2,0,1:T(8,128)} %copy-done.1) | copy-start | bytes 12582916
  207.1 1.0 copy-start.4
Sparse Core Ops, SparseCore 0:
  10.8 62.3 all-gather.3
  211.1 61.7 all-gather.5
